TPU v7x, 512 devices: a whole 4x4x16 slice. The times are simulated.
512 devices in a mesh: layer: 32 (over y, x, core), latent: 16 (over z).
Axes of the slice: x: 4, y: 4, z: 16, core: 2. Of those that a mesh axis runs over, the one named last changes fastest.
Arguments:
- layer_input: bfloat16 [32, 1024, 4096], P('layer', None, 'latent'), may hold values from -6 to 6
- enc_weight: bfloat16 [32, 4096, 2048], P('layer', None, 'latent'), may hold values from -0.09375 to 0.09375
- enc_bias: float32 [32, 2048], P('layer', 'latent'), may hold values from -3 to 3
- dec_weight: bfloat16 [32, 3, 2048, 4096], P('layer', None, None, 'latent'), may hold values from -0.25 to 0.25
- block_lists: int32 [32, 16, 8], P('layer'), may hold values from 0 to 15, as said below
- block_counts: int32 [32, 16], P('layer'), may hold values from 1 to 8, as said below
Outputs:
- rebuilt: bfloat16 [32, 1024, 4096], P('layer', None, 'latent')
Inputs may be any that keep to these rules, and one draw needn't show every extreme that they name: `block_lists`: each list holds distinct block ids of one layer. `block_counts`: some entry equals 8 in every draw.
All inputs are finite; a program needn't handle non-finite values.
Results may differ from a plain program's by a relative error of at most 0.0055.
Values may be sent and summed in bfloat16 or wider, within the bound.
A program may use at most 128 MiB of HBM per device.

v0:
```python
import jax
import jax.numpy as jnp
from jax import lax
from jax.sharding import PartitionSpec as P


def passed_along(value, axis, steps):
    count = lax.axis_size(axis)
    initial, last = (max(0, -steps), min(count, count - steps))
    return lax.ppermute(value, axis, [(source, source + steps) for source in range(initial, last)])


def shards(layer_input, enc_weight, enc_bias, dec_weight, block_lists, block_counts):
    encoder = enc_weight[0]
    tokens = layer_input.shape[1]
    block_width = encoder.shape[1]
    weight_rows = encoder
    preact = jnp.dot(
        lax.all_gather(layer_input, "latent", axis=2, tiled=True)[0],
        weight_rows,
        preferred_element_type=jnp.float32,
    )
    preact = preact + enc_bias[0][None, :]
    own_block = lax.axis_index("latent")
    active_ids = block_lists[0]
    counts = block_counts[0]
    slot_ids = jnp.arange(active_ids.shape[1])
    in_count = slot_ids[None, :] < counts[:, None]
    matched = (active_ids == own_block) & in_count
    tile_hit = jnp.any(matched, axis=1).astype(jnp.float32)
    tile_count = active_ids.shape[0]
    latent_act = (
        (
            jnp.maximum(preact, 0.0).reshape(tile_count, tokens // tile_count, block_width)
            * tile_hit[:, None, None]
        )
        .reshape(tokens, block_width)
        .astype(jnp.bfloat16)
    )
    decoder = dec_weight[0]
    targets = decoder.shape[0]
    weight_rows = decoder
    partials = jnp.einsum(
        "tk,skd->std",
        lax.all_gather(latent_act, "latent", axis=1, tiled=True),
        weight_rows,
        preferred_element_type=jnp.float32,
    )
    rebuilt = partials[0]
    for offset in range(1, targets):
        arrived = passed_along(partials[offset].astype(jnp.bfloat16), "layer", offset)
        rebuilt = rebuilt + arrived.astype(jnp.float32)
    return rebuilt.astype(jnp.bfloat16)[None]


def solution(mesh):
    placed = (
        P("layer", None, "latent"),
        P("layer", None, "latent"),
        P("layer", "latent"),
        P("layer", None, None, "latent"),
        P("layer", None, None),
        P("layer", None),
    )
    return jax.shard_map(
        shards, mesh=mesh, in_specs=placed, out_specs=P("layer", None, "latent"), check_vma=False
    )
```

profile of v0, /device:TPU:24, one launch (start us, length us, event | category | flops | bytes accessed | tf_op | source)
XLA Modules:
  0.0 273.7 jit_solution(11785571274011899842)
XLA Ops:
  6.5 0.0 copy-start
  6.5 0.0 all-gather.3.cloned.1.call-start
  6.5 0.7 all-gather.3.cloned.1.call-update
  7.3 0.0 all-gather.5.cloned.1.call-start
  7.3 0.9 fusion.28
  8.2 0.1 mul.13
  8.3 0.1 mul.14
  8.3 133.8 %all-gather.3.cloned.1.call-done = bf16[1,1024,4096]{2,1,0:T(8,128)(2,1)} async-done(((bf16[1,1024,256]{2,1,0:T(8,128)(2,1)}), bf16[1,1024,4096]{2,1,0:T(8,128)(2,1)}) %all-gather.3.cloned.1.call-update) | async-done | bytes 8388624 | tf_op jit(solution)/shard_map/all_gather | solution.py:19
  142.2 6.8 %fusion.19 = bf16[1024,128]{1,0:T(8,128)(2,1)} fusion(bf16[1,1024,4096]{2,1,0:T(8,128)(2,1)} %all-gather.3.cloned.1.call-done, bf16[1,4096,128]{2,1,0:T(8,128)(2,1)} %param.7, f32[1024]{0:T(1024)S(1)} %mul.14, f32[128]{0:T(128)} %bitcast.51), kind=kOutput, calls=%fused_computation.9 | convolution fusion | flops 1074266112 | bytes 9703936 | tf_op jit(solution)/shard_map/dot_general | solution.py:18
  149.0 0.0 all-gather.5.cloned.1.call-update
  149.0 90.9 %all-gather.5.cloned.1.call-done = bf16[1024,2048]{1,0:T(8,128)(2,1)} async-done(((bf16[1024,128]{1,0:T(8,128)(2,1)}), bf16[1024,2048]{1,0:T(8,128)(2,1)}) %all-gather.5.cloned.1.call-update) | async-done | bytes 4194320 | tf_op jit(solution)/shard_map/all_gather | solution.py:45
  239.9 0.0 copy-done
  239.9 5.2 %fusion.29 = (bf16[3,1024,256]{2,1,0:T(8,128)(2,1)S(1)}, f32[3,1024,256]{2,1,0:T(8,128)S(1)}) fusion(bf16[1,3,2048,256]{3,2,1,0:T(8,128)(2,1)S(1)} %copy-done, bf16[1024,2048]{1,0:T(8,128)(2,1)} %all-gather.5.cloned.1.call-done), kind=kOutput, calls=%fused_computation.21 | convolution fusion | flops 3222011904 | bytes 12058624 | tf_op jit(solution)/shard_map/tk,skd->std/dot_general | solution.py:43
  245.1 0.1 slice_bitcast_fusion.2
  245.1 1.9 collective-permute-start
  247.1 3.4 %collective-permute-start.1 = (bf16[1024,256]{1,0:T(8,128)(2,1)S(1)}, bf16[1024,256]{1,0:T(8,128)(2,1)S(1)}, u32[]{:S(2)}, u32[]{:S(2)}) collective-permute-start(bf16[1024,256]{1,0:T(8,128)(2,1)S(1)} %get-tuple-element.6), channel_id=1, source_target_pairs={{0,32},{16,48},{32,64},{48,80},{64,96},{80,112},{96,128},{112,144}... | collective-permute-start | bytes 1572872 | tf_op jit(solution)/shard_map/ppermute | solution.py:10
  250.5 10.4 %collective-permute-done = bf16[1024,256]{1,0:T(8,128)(2,1)S(1)} collective-permute-done((bf16[1024,256]{1,0:T(8,128)(2,1)S(1)}, bf16[1024,256]{1,0:T(8,128)(2,1)S(1)}, u32[]{:S(2)}, u32[]{:S(2)}) %collective-permute-start) | collective-permute-done | bytes 524320 | tf_op jit(solution)/shard_map/ppermute | solution.py:10
  260.9 5.0 %collective-permute-done.1 = bf16[1024,256]{1,0:T(8,128)(2,1)S(1)} collective-permute-done((bf16[1024,256]{1,0:T(8,128)(2,1)S(1)}, bf16[1024,256]{1,0:T(8,128)(2,1)S(1)}, u32[]{:S(2)}, u32[]{:S(2)}) %collective-permute-start.1) | collective-permute-done | bytes 524320 | tf_op jit(solution)/shard_map/ppermute | solution.py:10
  265.9 1.0 fusion.26
  (1 shorter events, 0.0 us)
Async XLA Ops:
  6.5 233.3 %copy-start = (bf16[1,3,2048,256]{3,2,1,0:T(8,128)(2,1)S(1)}, bf16[1,3,2048,256]{3,2,1,0:T(8,128)(2,1)}, u32[]{:S(2)}) copy-start(bf16[1,3,2048,256]{3,2,1,0:T(8,128)(2,1)} %param.9) | copy-start | bytes 9437188
  6.5 135.7 %all-gather.3.cloned.1.call-start = ((), (), s32[]{:S(2)}) async-start(), calls=%async_computation | async-start | bytes 8912896 | tf_op jit(solution)/shard_map/all_gather | solution.py:19
  7.3 232.6 %all-gather.5.cloned.1.call-start = ((), (), s32[]{:S(2)}) async-start(), calls=%async_computation.1 | async-start | bytes 4456448 | tf_op jit(solution)/shard_map/all_gather | solution.py:45
  245.1 15.7 %collective-permute-start = (bf16[1024,256]{1,0:T(8,128)(2,1)S(1)}, bf16[1024,256]{1,0:T(8,128)(2,1)S(1)}, u32[]{:S(2)}, u32[]{:S(2)}) collective-permute-start(bf16[1024,256]{1,0:T(8,128)(2,1)S(1)} %get-tuple-element.5), channel_id=1, source_target_pairs={{0,16},{16,32},{32,48},{48,64},{64,80},{80,96},{96,112},{112,128},... | collective-permute-start | bytes 1572872 | tf_op jit(solution)/shard_map/ppermute | solution.py:10
  247.1 18.8 %collective-permute-start.1 = (bf16[1024,256]{1,0:T(8,128)(2,1)S(1)}, bf16[1024,256]{1,0:T(8,128)(2,1)S(1)}, u32[]{:S(2)}, u32[]{:S(2)}) collective-permute-start(bf16[1024,256]{1,0:T(8,128)(2,1)S(1)} %get-tuple-element.6), channel_id=1, source_target_pairs={{0,32},{16,48},{32,64},{48,80},{64,96},{80,112},{96,128},{112,144}... | collective-permute-start | bytes 1572872 | tf_op jit(solution)/shard_map/ppermute | solution.py:10
Sparse Core Ops, SparseCore 0:
  9.3 132.8 all-gather.2
  149.1 90.7 all-gather.4
where the time goes:
time: 277 us; the launch traced here: 274 us
  waiting for transfers between devices  241 us (87%)
  between operations  13.4 us (5%)
  matrix products  12 us (4%)
  starting transfers between devices  5.34 us (2%)
    all_gather x1, waiting for transfers between devices, shards(): lax.all_gather(layer_input, 'latent', axis=2, tiled=True)[0]  134 us
    all_gather x1, waiting for transfers between devices, shards(): lax.all_gather(latent_act, 'latent', axis=1, tiled=True)  90.9 us
    ppermute x2, waiting for transfers between devices, passed_along(): lax.ppermute(value, axis, [(source, source + steps) for source in range(i...  15.4 us
    dot_general x1, matrix products, shards(): jnp.dot(lax.all_gather(layer_input, 'latent', axis=2, tiled=True)[0], wei...  6.77 us
  transfers between devices with their start and end apart: 4, of which 4 were waited for; matrix products, arithmetic and copies ran while one was open for 0% of the time, Pallas kernels for 0%

commit v1 on v0

v1 whole, which is shorter than its diff:
```python
import jax
import jax.numpy as jnp
from jax import lax
from jax.experimental import pallas as pl
from jax.experimental.pallas import tpu as pltpu
from jax.sharding import PartitionSpec as P

MESH = pl.DeviceIdType.MESH
BF16, F32 = jnp.bfloat16, jnp.float32
PIECES = 4


def kernel(
    x_hbm, enc_hbm, bias_ref, dec_hbm, lists, counts, out_ref,
    xv, wbuf, wd, pd, rs_in, rs_out, act, cur, dense, own, late, arrived, slot_of,
    load_sem, w_send, w_recv, rs_send, rs_recv, ag_send, ag_recv, out_send, out_recv,
):
    n, depth, blk = wbuf.shape
    tiles, tile = n, own.shape[1]
    slots = lists.shape[1]
    per = slots // PIECES
    targets = wd.shape[0]
    layers = lax.axis_size("layer")
    me, layer = lax.axis_index("latent"), lax.axis_index("layer")
    half = n // 2

    def ring(k):
        return lax.rem(k + 2 * n, n)

    load_x = pltpu.make_async_copy(x_hbm, xv, load_sem.at[0])
    load_w = pltpu.make_async_copy(enc_hbm.at[pl.ds(depth * me, depth)], wbuf.at[me], load_sem.at[1])
    load_d = pltpu.make_async_copy(dec_hbm, wd, load_sem.at[2])
    load_x.start()
    load_w.start()
    load_d.start()

    barrier = pltpu.get_barrier_semaphore()

    @pl.loop(1, n)
    def _(d):
        pl.semaphore_signal(barrier, inc=1, device_id={"latent": ring(me + d)}, device_id_type=MESH)

    expected = n - 1
    for j in range(1, targets):
        for delta in (j, -j):
            there = (layer + delta >= 0) & (layer + delta < layers)

            @pl.when(there)
            def _():
                pl.semaphore_signal(barrier, inc=1, device_id={"layer": layer + delta}, device_id_type=MESH)

            expected = expected + there.astype(jnp.int32)
    pl.semaphore_wait(barrier, expected)

    def shift(i):
        far = half - (i + 1) // 2
        return jnp.where(lax.rem(i, 2) == 1, far, n - far)

    def w_copy(i):
        to = ring(me + shift(i))
        return pltpu.make_async_remote_copy(
            src_ref=enc_hbm.at[pl.ds(pl.multiple_of(depth * to, depth), depth)],
            dst_ref=wbuf.at[me],
            send_sem=w_send.at[i], recv_sem=w_recv.at[i],
            device_id={"latent": to}, device_id_type=MESH,
        )

    def w_arrival(i):
        source = ring(me - shift(i))
        return source, pltpu.make_async_remote_copy(
            src_ref=wbuf.at[source], dst_ref=wbuf.at[source],
            send_sem=w_send.at[i], recv_sem=w_recv.at[i],
            device_id={"latent": source}, device_id_type=MESH,
        )

    @pl.loop(0, n - 1)
    def _(i):
        w_copy(i).start()

    @pl.loop(0, tiles)
    def _(t):
        @pl.loop(0, n)
        def _(b):
            found = jnp.int32(-1)
            for s in range(slots):
                hit = (lists[t, s] == b) & (s < counts[0, t])
                found = jnp.where(hit, s, found)
            slot_of[t, b] = found

    load_x.wait()
    load_w.wait()
    rows = xv.shape[0]
    chunk = min(rows, 256)

    def encode(source, bias):
        @pl.loop(0, rows // chunk)
        def _(c):
            part = pl.ds(pl.multiple_of(chunk * c, chunk), chunk)
            value = jnp.dot(xv[part], wbuf[source], preferred_element_type=F32)
            pd[source, part] = value if bias is None else value + bias

    encode(me, bias_ref[...])

    @pl.loop(0, n - 1)
    def _(i):
        source, copy = w_arrival(i)
        copy.wait_recv()
        encode(source, None)

    def hops(piece, way):
        return half if (piece < PIECES // 2) == (way == 0) else half - 1

    def tile_rows(t):
        return pl.ds(pl.multiple_of(tile * t, tile), tile)

    def partial(t, s):
        return pd[lists[t, s], tile_rows(t)]

    def neighbour(way):
        return {"latent": ring(me + (1 if way == 0 else -1))}

    def rs_copy(step, piece, way):
        part = pl.ds(per * piece, per)
        return pltpu.make_async_remote_copy(
            src_ref=rs_out.at[way, step, part], dst_ref=rs_in.at[way, step, part],
            send_sem=rs_send.at[way, step, piece], recv_sem=rs_recv.at[way, step, piece],
            device_id=neighbour(way), device_id_type=MESH,
        )

    def rs_step(step, first, last):
        for piece in range(PIECES):
            for way in (0, 1):
                count = hops(piece, way)
                if last and count < half:
                    continue
                t = ring(me + count - step) if way == 0 else ring(me - count + step)
                if not first:
                    rs_copy(step - 1, piece, way).wait_recv()
                for s in range(per * piece, per * piece + per):
                    value = partial(t, s)
                    if not first:
                        value = value + rs_in[way, step - 1, s].astype(F32)
                    rs_out[way, step, s] = value.astype(BF16)
                rs_copy(step, piece, way).start()

    rs_step(0, True, False)

    @pl.loop(1, half - 1)
    def _(step):
        rs_step(step, False, False)

    rs_step(half - 1, False, True)

    def ag_copy(step, piece, way):
        part = pl.ds(per * piece, per)
        t = ring(me - step) if way == 0 else ring(me + step)
        return pltpu.make_async_remote_copy(
            src_ref=act.at[t, part], dst_ref=act.at[t, part],
            send_sem=ag_send.at[way, step, piece], recv_sem=ag_recv.at[way, step, piece],
            device_id=neighbour(way), device_id_type=MESH,
        )

    def ag_arrival(step, piece, way):
        part = pl.ds(per * piece, per)
        t = ring(me - 1 - step) if way == 0 else ring(me + 1 + step)
        return pltpu.make_async_remote_copy(
            src_ref=act.at[t, part], dst_ref=act.at[t, part],
            send_sem=ag_send.at[way, step, piece], recv_sem=ag_recv.at[way, step, piece],
            device_id=neighbour(way), device_id_type=MESH,
        )

    for piece in range(PIECES):
        for way in (0, 1):
            rs_copy(hops(piece, way) - 1, piece, way).wait_recv()
        for s in range(per * piece, per * piece + per):
            value = partial(me, s)
            for way in (0, 1):
                value = value + rs_in[way, hops(piece, way) - 1, s].astype(F32)
            value = jnp.where(s < counts[0, me], jnp.maximum(value, 0.0), 0.0)
            act[me, s] = value.astype(BF16)
        for way in (0, 1):
            ag_copy(0, piece, way).start()

    load_d.wait()

    def out_copy(j, t):
        return pltpu.make_async_remote_copy(
            src_ref=late.at[j - 1, t], dst_ref=arrived.at[j - 1, t],
            send_sem=out_send.at[j - 1, t], recv_sem=out_recv.at[j - 1, t],
            device_id={"layer": lax.rem(layer + j, layers)}, device_id_type=MESH,
        )

    def decode(group):
        for k, t in enumerate(group):
            cur[...] = act[t]
            for b in range(n):
                slot = slot_of[t, b]
                value = cur[jnp.maximum(slot, 0)]
                value = jnp.where(slot >= 0, value, jnp.zeros_like(value))
                dense[k * tile : (k + 1) * tile, b * blk : (b + 1) * blk] = value
        m = len(group) * tile
        for j in range(targets):
            value = jnp.dot(dense[:m], wd[j], preferred_element_type=F32)
            for k, t in enumerate(group):
                mine = value[k * tile : (k + 1) * tile]
                if j == 0:
                    own[t] = mine
                else:
                    late[j - 1, t] = mine.astype(BF16)
            if j > 0:
                @pl.when(layer + j < layers)
                def _():
                    for t in group:
                        out_copy(j, t).start()

    decode([me])

    def ag_step(step, last):
        for piece in range(PIECES):
            for way in (0, 1):
                ag_arrival(step, piece, way).wait_recv()
                if not last or hops(piece, way) == half:
                    ag_copy(step + 1, piece, way).start()
        decode([ring(me - 1 - step), ring(me + 1 + step)])

    @pl.loop(0, half - 2)
    def _(step):
        ag_step(step, False)

    ag_step(half - 2, True)
    for piece in range(PIECES):
        for way in (0, 1):
            if hops(piece, way) == half:
                ag_arrival(half - 1, piece, way).wait_recv()
    decode([ring(me + half)])

    for j in range(1, targets):
        @pl.when(layer < j)
        def _():
            arrived[j - 1] = jnp.zeros(arrived.shape[1:], BF16)

    @pl.loop(0, tiles)
    def _(i):
        t = ring(me + jnp.where(lax.rem(i, 2) == 1, (i + 1) // 2, n - i // 2))
        for j in range(1, targets):
            @pl.when(layer >= j)
            def _():
                out_copy(j, t).wait_recv()
        value = own[t]
        for j in range(1, targets):
            value = value + arrived[j - 1, t].astype(F32)
        out_ref[tile_rows(t)] = value.astype(BF16)

    @pl.loop(0, n - 1)
    def _(i):
        w_copy(i).wait_send()

    def drain(step, last):
        for piece in range(PIECES):
            for way in (0, 1):
                if not last or hops(piece, way) == half:
                    rs_copy(step, piece, way).wait_send()
                    ag_copy(step, piece, way).wait_send()

    @pl.loop(0, half - 1)
    def _(step):
        drain(step, False)

    drain(half - 1, True)

    @pl.loop(0, tiles)
    def _(t):
        for j in range(1, targets):
            @pl.when(layer + j < layers)
            def _():
                out_copy(j, t).wait_send()


def shards(layer_input, enc_weight, enc_bias, dec_weight, block_lists, block_counts):
    x, enc, dec = layer_input[0], enc_weight[0], dec_weight[0]
    tokens, depth = x.shape
    blk = enc.shape[1]
    targets, _, feats = dec.shape
    tiles, slots = block_lists.shape[1:]
    n = lax.axis_size("latent")
    tile, half = tokens // tiles, n // 2
    anywhere = pl.BlockSpec(memory_space=pl.ANY)
    vmem = pl.BlockSpec(memory_space=pltpu.VMEM)
    smem = pl.BlockSpec(memory_space=pltpu.SMEM)
    dma = pltpu.SemaphoreType.DMA
    out = pl.pallas_call(
        kernel,
        out_shape=jax.ShapeDtypeStruct((tokens, feats), BF16),
        in_specs=[anywhere, anywhere, vmem, anywhere, smem, smem],
        out_specs=vmem,
        scratch_shapes=[
            pltpu.VMEM((tokens, depth), BF16),
            pltpu.VMEM((n, depth, blk), BF16),
            pltpu.VMEM(dec.shape, BF16),
            pltpu.VMEM((n, tokens, blk), F32),
            pltpu.VMEM((2, half, slots, tile, blk), BF16),
            pltpu.VMEM((2, half, slots, tile, blk), BF16),
            pltpu.VMEM((tiles, slots, tile, blk), BF16),
            pltpu.VMEM((slots, tile, blk), BF16),
            pltpu.VMEM((2 * tile, n * blk), BF16),
            pltpu.VMEM((tiles, tile, feats), F32),
            pltpu.VMEM((targets - 1, tiles, tile, feats), BF16),
            pltpu.VMEM((targets - 1, tiles, tile, feats), BF16),
            pltpu.SMEM((tiles, n), jnp.int32),
            dma((3,)),
            dma((n - 1,)),
            dma((n - 1,)),
            dma((2, half, PIECES)),
            dma((2, half, PIECES)),
            dma((2, half, PIECES)),
            dma((2, half, PIECES)),
            dma((targets - 1, tiles)),
            dma((targets - 1, tiles)),
        ],
        compiler_params=pltpu.CompilerParams(
            collective_id=0, has_side_effects=True, vmem_limit_bytes=48 << 20
        ),
        cost_estimate=pl.CostEstimate(
            flops=2 * tokens * n * blk * (depth + targets * feats),
            bytes_accessed=2 * (x.size + 2 * enc.size + dec.size + tokens * feats),
            transcendentals=0,
        ),
        name="transcoder",
    )(x, enc, enc_bias, dec, block_lists[0], block_counts)
    return out[None]


def solution(mesh):
    placed = (
        P("layer", None, "latent"),
        P("layer", None, "latent"),
        P("layer", "latent"),
        P("layer", None, None, "latent"),
        P("layer", None, None),
        P("layer", None),
    )
    return jax.shard_map(
        shards, mesh=mesh, in_specs=placed, out_specs=P("layer", None, "latent"), check_vma=False
    )
```

time: 277 us -> 137 us (0.49)
  waiting for transfers between devices: 241 us -> 0 us
  Pallas kernels: 0 us -> 129 us
  between operations: 13.4 us -> 0.01 us
  matrix products: 12 us -> 0 us
  local copies, waits for them, and re-layouts: 0.22 us -> 7.02 us
  starting transfers between devices: 5.34 us -> 0 us
    all_gather x2 -> x0, waiting for transfers between devices: 225 us -> none  [the longest x1 134 us: shards(): lax.all_gather(layer_input, 'latent', axis=2, tiled=True)[0]]
    pallas_call x0 -> x1, Pallas kernels: none -> 129 us  [shards(): pl.pallas_call(kernel, out_shape=jax.ShapeDtypeStruct((tokens, feats), BF...]
    ppermute x2 -> x0, waiting for transfers between devices: 15.4 us -> none  [passed_along(): lax.ppermute(value, axis, [(source, source + steps) for source in range(i...]
    dot_general x2 -> x0, matrix products: 12 us -> none  [the longest x1 6.77 us: shards(): jnp.dot(lax.all_gather(layer_input, 'latent', axis=2, tiled=True)[0], wei...]
    unnamed x2 -> x11, local copies, waits for them, and re-layouts: 0.01 us -> 6.26 us
    ppermute x2 -> x0, starting transfers between devices: 5.3 us -> none  [passed_along(): lax.ppermute(value, axis, [(source, source + steps) for source in range(i...]
  transfers between devices with their start and end apart: 4 -> 0, of which waited for: 4 -> 0; matrix products, arithmetic and copies ran while one was open for 0% -> 0% of each run, Pallas kernels for 0% -> 0%
where the time goes in v1:
time: 137 us; the launch traced here: 136 us
  Pallas kernels  129 us (94%)
  local copies, waits for them, and re-layouts  7.02 us (5%)
    pallas_call x1, Pallas kernels, shards(): pl.pallas_call(kernel, out_shape=jax.ShapeDtypeStruct((tokens, feats), BF...  129 us
    unnamed x11, local copies, waits for them, and re-layouts  6.26 us

profile of v1, /device:TPU:24, one launch (start us, length us, event | category | flops | bytes accessed | tf_op | source)
XLA Modules:
  0.0 136.5 jit_solution(398794497448727417)
XLA Ops:
  0.0 0.8 copy.7.lists
  0.8 0.0 copy-start
  0.8 1.9 %copy-done = bf16[1,3,2048,256]{3,2,1,0:T(8,128)(2,1)S(1)} copy-done((bf16[1,3,2048,256]{3,2,1,0:T(8,128)(2,1)S(1)}, bf16[1,3,2048,256]{3,2,1,0:T(8,128)(2,1)}, u32[]{:S(2)}) %copy-start) | copy-done | bytes 3145752
  2.6 0.0 copy-start.1
  2.6 1.2 copy-done.1
  3.9 0.0 copy-start.2
  3.9 1.0 copy-done.2
  4.9 0.0 copy-start.3
  4.9 0.7 copy-done.3
  5.6 0.0 copy-start.4
  5.6 0.7 copy-done.4
  6.2 129.4 %transcoder.1 = bf16[1024,256]{1,0:T(8,128)(2,1)S(1)} custom-call(bf16[1024,256]{1,0:T(8,128)(2,1)S(1)} %bitcast.8, bf16[4096,128]{1,0:T(8,128)(2,1)S(1)} %bitcast.7, f32[1,128]{1,0:T(1,128)S(1)} %copy-done.3, bf16[3,2048,256]{2,1,0:T(8,128)(2,1)S(1)} %bitcast.6, s32[16,8]{1,0:T(8,128)S(1)} %copy.7.lists, s32[1,16]{1,0:T(1,128)S(1)} %copy-done.4), custom_call_target="tpu_custom_call" | custom-call | flops 4294967296 | bytes 6291456 | tf_op jit(solution)/shard_map/transcoder/pallas_call | solution.py:291
  135.7 0.8 copy.9
Async XLA Ops:
  0.8 1.9 %copy-start = (bf16[1,3,2048,256]{3,2,1,0:T(8,128)(2,1)S(1)}, bf16[1,3,2048,256]{3,2,1,0:T(8,128)(2,1)}, u32[]{:S(2)}) copy-start(bf16[1,3,2048,256]{3,2,1,0:T(8,128)(2,1)} %param.9) | copy-start | bytes 9437188
  2.6 1.2 copy-start.1
  3.9 1.0 copy-start.2
  4.9 0.7 copy-start.3
  5.6 0.7 copy-start.4

commit v2 on v1

--- a/solution.py
+++ b/solution.py
@@ -17,7 +17,7 @@
 ):
     n, depth, blk = wbuf.shape
     tiles, tile = n, own.shape[1]
-    slots = lists.shape[1]
+    slots = lists.shape[0]
     per = slots // PIECES
     targets = wd.shape[0]
     layers = lax.axis_size("layer")
@@ -83,7 +83,7 @@
         def _(b):
             found = jnp.int32(-1)
             for s in range(slots):
-                hit = (lists[t, s] == b) & (s < counts[0, t])
+                hit = (lists[s, t] == b) & (s < counts[0, t])
                 found = jnp.where(hit, s, found)
             slot_of[t, b] = found
 
@@ -107,75 +107,91 @@
         copy.wait_recv()
         encode(source, None)
 
-    def hops(piece, way):
-        return half if (piece < PIECES // 2) == (way == 0) else half - 1
+    def from_opposite(piece, way):
+        return (piece < PIECES // 2) == (way == 0)
 
     def tile_rows(t):
         return pl.ds(pl.multiple_of(tile * t, tile), tile)
 
     def partial(t, s):
-        return pd[lists[t, s], tile_rows(t)]
-
-    def neighbour(way):
-        return {"latent": ring(me + (1 if way == 0 else -1))}
+        return pd[lists[s, t], tile_rows(t)]
+
+    def toward(way, count):
+        return ring(me + count if way == 0 else me - count)
+
+    def hop(source, target, sends, recvs, index, way, count):
+        return pltpu.make_async_remote_copy(
+            src_ref=source, dst_ref=target, send_sem=sends.at[index], recv_sem=recvs.at[index],
+            device_id={"latent": toward(way, count)}, device_id_type=MESH,
+        )
+
+    def slots_of(piece):
+        return range(per * piece, per * piece + per)
 
     def rs_copy(step, piece, way):
         part = pl.ds(per * piece, per)
-        return pltpu.make_async_remote_copy(
-            src_ref=rs_out.at[way, step, part], dst_ref=rs_in.at[way, step, part],
-            send_sem=rs_send.at[way, step, piece], recv_sem=rs_recv.at[way, step, piece],
-            device_id=neighbour(way), device_id_type=MESH,
-        )
-
-    def rs_step(step, first, last):
+        return hop(rs_out.at[way, step, part], rs_in.at[way, step, part], rs_send, rs_recv, (way, step, piece), way, 1)
+
+    last = half - 1
+
+    def rs_jump(piece, way):
+        part = pl.ds(per * piece, per)
+        return hop(rs_out.at[way, last, part], rs_in.at[way, last, part], rs_send, rs_recv, (way, last, piece), way, 2)
+
+    for piece in range(PIECES):
+        for way in (0, 1):
+            if from_opposite(piece, way):
+                for s in slots_of(piece):
+                    rs_out[way, last, s] = partial(ring(me + half), s).astype(BF16)
+                rs_jump(piece, way).start()
+
+    def rs_step(step, before, joined):
         for piece in range(PIECES):
             for way in (0, 1):
-                count = hops(piece, way)
-                if last and count < half:
-                    continue
-                t = ring(me + count - step) if way == 0 else ring(me - count + step)
-                if not first:
+                if before:
                     rs_copy(step - 1, piece, way).wait_recv()
-                for s in range(per * piece, per * piece + per):
-                    value = partial(t, s)
-                    if not first:
+                join = joined and from_opposite(piece, way)
+                if join:
+                    rs_jump(piece, way).wait_recv()
+                for s in slots_of(piece):
+                    value = partial(toward(way, last - step), s)
+                    if before:
                         value = value + rs_in[way, step - 1, s].astype(F32)
+                    if join:
+                        value = value + rs_in[way, last, s].astype(F32)
                     rs_out[way, step, s] = value.astype(BF16)
                 rs_copy(step, piece, way).start()
 
-    rs_step(0, True, False)
-
-    @pl.loop(1, half - 1)
+    rs_step(0, False, False)
+    rs_step(1, True, True)
+
+    @pl.loop(2, last)
     def _(step):
-        rs_step(step, False, False)
-
-    rs_step(half - 1, False, True)
+        rs_step(step, True, False)
+
+    def act_copy(t, piece, index, way, count):
+        here = act.at[t, pl.ds(per * piece, per)]
+        return hop(here, here, ag_send, ag_recv, index, way, count)
 
     def ag_copy(step, piece, way):
-        part = pl.ds(per * piece, per)
-        t = ring(me - step) if way == 0 else ring(me + step)
-        return pltpu.make_async_remote_copy(
-            src_ref=act.at[t, part], dst_ref=act.at[t, part],
-            send_sem=ag_send.at[way, step, piece], recv_sem=ag_recv.at[way, step, piece],
-            device_id=neighbour(way), device_id_type=MESH,
-        )
+        return act_copy(toward(1 - way, step), piece, (way, step, piece), way, 1)
 
     def ag_arrival(step, piece, way):
-        part = pl.ds(per * piece, per)
-        t = ring(me - 1 - step) if way == 0 else ring(me + 1 + step)
-        return pltpu.make_async_remote_copy(
-            src_ref=act.at[t, part], dst_ref=act.at[t, part],
-            send_sem=ag_send.at[way, step, piece], recv_sem=ag_recv.at[way, step, piece],
-            device_id=neighbour(way), device_id_type=MESH,
-        )
+        return act_copy(toward(1 - way, step + 1), piece, (way, step, piece), way, 1)
+
+    def ag_jump(piece, way):
+        return act_copy(toward(1 - way, last - 1), piece, (way, last, piece), way, 2)
+
+    def ag_jumped(piece, way):
+        return act_copy(ring(me + half), piece, (way, last, piece), way, 2)
 
     for piece in range(PIECES):
         for way in (0, 1):
-            rs_copy(hops(piece, way) - 1, piece, way).wait_recv()
-        for s in range(per * piece, per * piece + per):
+            rs_copy(last - 1, piece, way).wait_recv()
+        for s in slots_of(piece):
             value = partial(me, s)
             for way in (0, 1):
-                value = value + rs_in[way, hops(piece, way) - 1, s].astype(F32)
+                value = value + rs_in[way, last - 1, s].astype(F32)
             value = jnp.where(s < counts[0, me], jnp.maximum(value, 0.0), 0.0)
             act[me, s] = value.astype(BF16)
         for way in (0, 1):
@@ -215,24 +231,26 @@
 
     decode([me])
 
-    def ag_step(step, last):
+    def ag_step(step, jump):
         for piece in range(PIECES):
             for way in (0, 1):
                 ag_arrival(step, piece, way).wait_recv()
-                if not last or hops(piece, way) == half:
-                    ag_copy(step + 1, piece, way).start()
-        decode([ring(me - 1 - step), ring(me + 1 + step)])
-
-    @pl.loop(0, half - 2)
+                ag_copy(step + 1, piece, way).start()
+                if jump and from_opposite(piece, way):
+                    ag_jump(piece, way).start()
+        decode([toward(1, step + 1), toward(0, step + 1)])
+
+    @pl.loop(0, last - 2)
     def _(step):
         ag_step(step, False)
 
-    ag_step(half - 2, True)
+    ag_step(last - 2, True)
     for piece in range(PIECES):
         for way in (0, 1):
-            if hops(piece, way) == half:
-                ag_arrival(half - 1, piece, way).wait_recv()
-    decode([ring(me + half)])
+            ag_arrival(last - 1, piece, way).wait_recv()
+            if from_opposite(piece, way):
+                ag_jumped(piece, way).wait_recv()
+    decode([toward(1, last), toward(0, last), ring(me + half)])
 
     for j in range(1, targets):
         @pl.when(layer < j)
@@ -255,18 +273,18 @@
     def _(i):
         w_copy(i).wait_send()
 
-    def drain(step, last):
+    @pl.loop(0, last)
+    def _(step):
         for piece in range(PIECES):
             for way in (0, 1):
-                if not last or hops(piece, way) == half:
-                    rs_copy(step, piece, way).wait_send()
-                    ag_copy(step, piece, way).wait_send()
-
-    @pl.loop(0, half - 1)
-    def _(step):
-        drain(step, False)
-
-    drain(half - 1, True)
+                rs_copy(step, piece, way).wait_send()
+                ag_copy(step, piece, way).wait_send()
+
+    for piece in range(PIECES):
+        for way in (0, 1):
+            if from_opposite(piece, way):
+                rs_jump(piece, way).wait_send()
+                ag_jump(piece, way).wait_send()
 
     @pl.loop(0, tiles)
     def _(t):
@@ -284,14 +302,14 @@
     tiles, slots = block_lists.shape[1:]
     n = lax.axis_size("latent")
     tile, half = tokens // tiles, n // 2
-    anywhere = pl.BlockSpec(memory_space=pl.ANY)
+    hbm = pl.BlockSpec(memory_space=pltpu.HBM)
     vmem = pl.BlockSpec(memory_space=pltpu.VMEM)
     smem = pl.BlockSpec(memory_space=pltpu.SMEM)
     dma = pltpu.SemaphoreType.DMA
     out = pl.pallas_call(
         kernel,
         out_shape=jax.ShapeDtypeStruct((tokens, feats), BF16),
-        in_specs=[anywhere, anywhere, vmem, anywhere, smem, smem],
+        in_specs=[hbm, hbm, vmem, hbm, smem, smem],
         out_specs=vmem,
         scratch_shapes=[
             pltpu.VMEM((tokens, depth), BF16),
@@ -302,7 +320,7 @@
             pltpu.VMEM((2, half, slots, tile, blk), BF16),
             pltpu.VMEM((tiles, slots, tile, blk), BF16),
             pltpu.VMEM((slots, tile, blk), BF16),
-            pltpu.VMEM((2 * tile, n * blk), BF16),
+            pltpu.VMEM((3 * tile, n * blk), BF16),
             pltpu.VMEM((tiles, tile, feats), F32),
             pltpu.VMEM((targets - 1, tiles, tile, feats), BF16),
             pltpu.VMEM((targets - 1, tiles, tile, feats), BF16),
@@ -318,7 +336,7 @@
             dma((targets - 1, tiles)),
         ],
         compiler_params=pltpu.CompilerParams(
-            collective_id=0, has_side_effects=True, vmem_limit_bytes=48 << 20
+            collective_id=0, has_side_effects=True, vmem_limit_bytes=67000000
         ),
         cost_estimate=pl.CostEstimate(
             flops=2 * tokens * n * blk * (depth + targets * feats),
@@ -326,7 +344,7 @@
             transcendentals=0,
         ),
         name="transcoder",
-    )(x, enc, enc_bias, dec, block_lists[0], block_counts)
+    )(x, enc, enc_bias, dec, block_lists[0].T, block_counts)
     return out[None]
 
 

time: 137 us -> 133 us (0.971)
  local copies, waits for them, and re-layouts: 7.02 us -> 1.87 us
  Pallas kernels: 129 us -> 131 us
    unnamed x11 -> x1, local copies, waits for them, and re-layouts: 6.26 us -> 1.87 us
    pallas_call x1, Pallas kernels: 129 us -> 131 us  [shards(): pl.pallas_call(kernel, out_shape=jax.ShapeDtypeStruct((tokens, feats), BF...]
where the time goes in v2:
time: 133 us
  Pallas kernels  131 us (98%)
  local copies, waits for them, and re-layouts  1.87 us (1%)
    pallas_call x1, Pallas kernels, shards(): pl.pallas_call(kernel, out_shape=jax.ShapeDtypeStruct((tokens, feats), BF...  131 us

profile of v2, /device:TPU:24, one launch (start us, length us, event | category | flops | bytes accessed | tf_op | source)
XLA Modules:
  0.0 132.9 jit_solution(13018563289574903503)
XLA Ops:
  0.0 131.0 %transcoder.1 = bf16[1024,256]{1,0:T(8,128)(2,1)} custom-call(bf16[1024,256]{1,0:T(8,128)(2,1)} %bitcast.10, bf16[4096,128]{1,0:T(8,128)(2,1)} %bitcast.9, f32[1,128]{1,0:T(1,128)} %bias_ref.1, bf16[3,2048,256]{2,1,0:T(8,128)(2,1)} %bitcast.8, s32[8,16]{1,0:T(8,128)} %bitcast.11, s32[1,16]{1,0:T(1,128)} %counts.1), custom_call_target="tpu_custom_call" | custom-call | flops 4294967296 | bytes 6291456 | tf_op jit(solution)/shard_map/transcoder/pallas_call | solution.py:309
  131.0 1.9 %copy.8 = bf16[1,1024,256]{2,1,0:T(8,128)(2,1)} copy(bf16[1,1024,256]{2,1,0:T(8,128)(2,1)} %bitcast.7) | data formatting | bytes 1048576

commit v3 on v2

--- a/solution.py
+++ b/solution.py
@@ -11,9 +11,9 @@
 
 
 def kernel(
-    x_hbm, enc_hbm, bias_ref, dec_hbm, lists, counts, out_ref,
-    xv, wbuf, wd, pd, rs_in, rs_out, act, cur, dense, own, late, arrived, slot_of,
-    load_sem, w_send, w_recv, rs_send, rs_recv, ag_send, ag_recv, out_send, out_recv,
+    x_hbm, enc_hbm, bias_ref, dec_hbm, lists, counts, own_out, arrived,
+    xv, wbuf, wd, pd, rs_in, rs_out, act, cur, dense, own, late, slot_of,
+    load_sem, w_send, w_recv, rs_send, rs_recv, ag_send, ag_recv, out_send, out_recv, own_sem,
 ):
     n, depth, blk = wbuf.shape
     tiles, tile = n, own.shape[1]
@@ -206,68 +206,69 @@
             device_id={"layer": lax.rem(layer + j, layers)}, device_id_type=MESH,
         )
 
+    def own_copy(t):
+        return pltpu.make_async_copy(own.at[t], own_out.at[t], own_sem.at[t])
+
     def decode(group):
         for k, t in enumerate(group):
             cur[...] = act[t]
-            for b in range(n):
+
+            @pl.loop(0, n, unroll=2)
+            def _(b):
                 slot = slot_of[t, b]
                 value = cur[jnp.maximum(slot, 0)]
                 value = jnp.where(slot >= 0, value, jnp.zeros_like(value))
-                dense[k * tile : (k + 1) * tile, b * blk : (b + 1) * blk] = value
-        m = len(group) * tile
-        for j in range(targets):
-            value = jnp.dot(dense[:m], wd[j], preferred_element_type=F32)
+                dense[k * tile : (k + 1) * tile, pl.ds(pl.multiple_of(b * blk, blk), blk)] = value
+
+        def term(j):
+            return jnp.dot(dense[...], wd[j], preferred_element_type=F32)
+
+        @pl.loop(1, targets)
+        def _(j):
+            value = term(j)
             for k, t in enumerate(group):
-                mine = value[k * tile : (k + 1) * tile]
-                if j == 0:
-                    own[t] = mine
-                else:
-                    late[j - 1, t] = mine.astype(BF16)
-            if j > 0:
-                @pl.when(layer + j < layers)
-                def _():
-                    for t in group:
-                        out_copy(j, t).start()
-
-    decode([me])
-
-    def ag_step(step, jump):
+                late[j - 1, t] = value[k * tile : (k + 1) * tile].astype(BF16)
+
+            @pl.when(layer + j < layers)
+            def _():
+                for t in group:
+                    out_copy(j, t).start()
+
+        value = term(0)
+        for k, t in enumerate(group):
+            own[t] = value[k * tile : (k + 1) * tile]
+            own_copy(t).start()
+
+    @pl.loop(0, half)
+    def _(step):
         for piece in range(PIECES):
             for way in (0, 1):
-                ag_arrival(step, piece, way).wait_recv()
-                ag_copy(step + 1, piece, way).start()
-                if jump and from_opposite(piece, way):
-                    ag_jump(piece, way).start()
-        decode([toward(1, step + 1), toward(0, step + 1)])
-
-    @pl.loop(0, last - 2)
-    def _(step):
-        ag_step(step, False)
-
-    ag_step(last - 2, True)
-    for piece in range(PIECES):
-        for way in (0, 1):
-            ag_arrival(last - 1, piece, way).wait_recv()
-            if from_opposite(piece, way):
-                ag_jumped(piece, way).wait_recv()
-    decode([toward(1, last), toward(0, last), ring(me + half)])
-
-    for j in range(1, targets):
-        @pl.when(layer < j)
-        def _():
-            arrived[j - 1] = jnp.zeros(arrived.shape[1:], BF16)
+                @pl.when(step < last)
+                def _():
+                    ag_arrival(step, piece, way).wait_recv()
+
+                @pl.when(step < last - 1)
+                def _():
+                    ag_copy(step + 1, piece, way).start()
+
+                if from_opposite(piece, way):
+                    @pl.when(step == last - 2)
+                    def _():
+                        ag_jump(piece, way).start()
+
+                    @pl.when(step == last)
+                    def _():
+                        ag_jumped(piece, way).wait_recv()
+
+        decode([toward(1, step + 1), toward(0, lax.rem(step + 1, half))])
 
     @pl.loop(0, tiles)
-    def _(i):
-        t = ring(me + jnp.where(lax.rem(i, 2) == 1, (i + 1) // 2, n - i // 2))
+    def _(t):
+        own_copy(t).wait()
         for j in range(1, targets):
             @pl.when(layer >= j)
             def _():
                 out_copy(j, t).wait_recv()
-        value = own[t]
-        for j in range(1, targets):
-            value = value + arrived[j - 1, t].astype(F32)
-        out_ref[tile_rows(t)] = value.astype(BF16)
 
     @pl.loop(0, n - 1)
     def _(i):
@@ -306,11 +307,14 @@
     vmem = pl.BlockSpec(memory_space=pltpu.VMEM)
     smem = pl.BlockSpec(memory_space=pltpu.SMEM)
     dma = pltpu.SemaphoreType.DMA
-    out = pl.pallas_call(
+    own, arrived = pl.pallas_call(
         kernel,
-        out_shape=jax.ShapeDtypeStruct((tokens, feats), BF16),
+        out_shape=[
+            jax.ShapeDtypeStruct((tiles, tile, feats), F32),
+            jax.ShapeDtypeStruct((targets - 1, tiles, tile, feats), BF16),
+        ],
         in_specs=[hbm, hbm, vmem, hbm, smem, smem],
-        out_specs=vmem,
+        out_specs=[hbm, hbm],
         scratch_shapes=[
             pltpu.VMEM((tokens, depth), BF16),
             pltpu.VMEM((n, depth, blk), BF16),
@@ -320,9 +324,8 @@
             pltpu.VMEM((2, half, slots, tile, blk), BF16),
             pltpu.VMEM((tiles, slots, tile, blk), BF16),
             pltpu.VMEM((slots, tile, blk), BF16),
-            pltpu.VMEM((3 * tile, n * blk), BF16),
+            pltpu.VMEM((2 * tile, n * blk), BF16),
             pltpu.VMEM((tiles, tile, feats), F32),
-            pltpu.VMEM((targets - 1, tiles, tile, feats), BF16),
             pltpu.VMEM((targets - 1, tiles, tile, feats), BF16),
             pltpu.SMEM((tiles, n), jnp.int32),
             dma((3,)),
@@ -334,9 +337,10 @@
             dma((2, half, PIECES)),
             dma((targets - 1, tiles)),
             dma((targets - 1, tiles)),
+            dma((tiles,)),
         ],
         compiler_params=pltpu.CompilerParams(
-            collective_id=0, has_side_effects=True, vmem_limit_bytes=67000000
+            collective_id=0, has_side_effects=True, vmem_limit_bytes=40 << 20
         ),
         cost_estimate=pl.CostEstimate(
             flops=2 * tokens * n * blk * (depth + targets * feats),
@@ -344,8 +348,13 @@
             transcendentals=0,
         ),
         name="transcoder",
-    )(x, enc, enc_bias, dec, block_lists[0].T, block_counts)
-    return out[None]
+    )(*(pltpu.with_memory_space_constraint(a, pltpu.HBM) for a in (x, enc, enc_bias, dec, block_lists[0].T, block_counts)))
+    layer = lax.axis_index("layer")
+    rebuilt = own
+    for j in range(1, targets):
+        term = arrived[j - 1].astype(F32)
+        rebuilt = rebuilt + jnp.where(layer >= j, term, 0.0)
+    return rebuilt.astype(BF16).reshape(1, tokens, feats)
 
 
 def solution(mesh):

time: 133 us -> 132 us (level)
  local copies, waits for them, and re-layouts: 1.87 us -> 0 us
    unnamed x1 -> x0, local copies, waits for them, and re-layouts: 1.87 us -> none
where the time goes in v3:
time: 132 us
  Pallas kernels  131 us (99%)
    pallas_call x1, Pallas kernels, shards(): pl.pallas_call(kernel, out_shape=[jax.ShapeDtypeStruct((tiles, tile, feat...  131 us

profile of v3, /device:TPU:24, one launch (start us, length us, event | category | flops | bytes accessed | tf_op | source)
XLA Modules:
  0.0 131.8 jit_solution(12375989642571106147)
XLA Ops:
  0.0 130.7 %transcoder.1 = (f32[16,64,256]{2,1,0:T(8,128)S(1)}, bf16[2,16,64,256]{3,2,1,0:T(8,128)(2,1)S(1)}) custom-call(bf16[1024,256]{1,0:T(8,128)(2,1)} %bitcast.17, bf16[4096,128]{1,0:T(8,128)(2,1)} %bitcast.16, f32[1,128]{1,0:T(1,128)} %bias_ref.1, bf16[3,2048,256]{2,1,0:T(8,128)(2,1)} %bitcast.15, s32[8,16]{1,0:T(8,128)} %bitcast.18, s32[1,16]{1,0:T(1,128)} %counts.1), custom_call_target="tpu_custom_call" | custom-call | flops 4294967296 | bytes 6291456 | tf_op jit(solution)/shard_map/transcoder/pallas_call | solution.py:310
  130.7 1.0 fusion

commit v4 on v3

--- a/solution.py
+++ b/solution.py
@@ -25,7 +25,8 @@
     half = n // 2
 
     def ring(k):
-        return lax.rem(k + 2 * n, n)
+        k = jnp.where(k >= n, k - n, k)
+        return jnp.where(k < 0, k + n, k)
 
     load_x = pltpu.make_async_copy(x_hbm, xv, load_sem.at[0])
     load_w = pltpu.make_async_copy(enc_hbm.at[pl.ds(depth * me, depth)], wbuf.at[me], load_sem.at[1])
@@ -119,10 +120,12 @@
     def toward(way, count):
         return ring(me + count if way == 0 else me - count)
 
+    beside = [[toward(way, count) for count in (1, 2)] for way in (0, 1)]
+
     def hop(source, target, sends, recvs, index, way, count):
         return pltpu.make_async_remote_copy(
             src_ref=source, dst_ref=target, send_sem=sends.at[index], recv_sem=recvs.at[index],
-            device_id={"latent": toward(way, count)}, device_id_type=MESH,
+            device_id={"latent": beside[way][count - 1]}, device_id_type=MESH,
         )
 
     def slots_of(piece):
@@ -203,7 +206,7 @@
         return pltpu.make_async_remote_copy(
             src_ref=late.at[j - 1, t], dst_ref=arrived.at[j - 1, t],
             send_sem=out_send.at[j - 1, t], recv_sem=out_recv.at[j - 1, t],
-            device_id={"layer": lax.rem(layer + j, layers)}, device_id_type=MESH,
+            device_id={"layer": jnp.where(layer + j >= layers, layer + j - layers, layer + j)}, device_id_type=MESH,
         )
 
     def own_copy(t):
@@ -260,7 +263,7 @@
                     def _():
                         ag_jumped(piece, way).wait_recv()
 
-        decode([toward(1, step + 1), toward(0, lax.rem(step + 1, half))])
+        decode([toward(1, step + 1), toward(0, jnp.where(step == last, 0, step + 1))])
 
     @pl.loop(0, tiles)
     def _(t):

time: 132 us -> 132 us (level)
  no operation moved by 1% of the time
where the time goes in v4:
time: 132 us
  Pallas kernels  131 us (99%)
    pallas_call x1, Pallas kernels, shards(): pl.pallas_call(kernel, out_shape=[jax.ShapeDtypeStruct((tiles, tile, feat...  131 us

profile of v4, /device:TPU:24, one launch (start us, length us, event | category | flops | bytes accessed | tf_op | source)
XLA Modules:
  0.0 131.8 jit_solution(4731106448685722327)
XLA Ops:
  0.0 130.7 %transcoder.1 = (f32[16,64,256]{2,1,0:T(8,128)S(1)}, bf16[2,16,64,256]{3,2,1,0:T(8,128)(2,1)S(1)}) custom-call(bf16[1024,256]{1,0:T(8,128)(2,1)} %bitcast.17, bf16[4096,128]{1,0:T(8,128)(2,1)} %bitcast.16, f32[1,128]{1,0:T(1,128)} %bias_ref.1, bf16[3,2048,256]{2,1,0:T(8,128)(2,1)} %bitcast.15, s32[8,16]{1,0:T(8,128)} %bitcast.18, s32[1,16]{1,0:T(1,128)} %counts.1), custom_call_target="tpu_custom_call" | custom-call | flops 4294967296 | bytes 6291456 | tf_op jit(solution)/shard_map/transcoder/pallas_call | solution.py:313
  130.7 1.0 fusion
